TPU v7x, 32 devices: a whole 2x2x4 slice. The times are simulated.
32 devices in a mesh: dp: 4 (over x, core), blk: 4 (over z), inner: 2 (over y).
Axes of the slice: x: 2, y: 2, z: 4, core: 2. Of those that a mesh axis runs over, the one named last changes fastest.
Arguments:
- queries: bfloat16 [4, 1024, 1536], P('dp', ('blk', 'inner')), may hold values from -6 to 6
- keys: bfloat16 [4, 1024, 1536], P('dp', ('blk', 'inner')), may hold values from -6 to 6
- values: bfloat16 [4, 1024, 1536], P('dp', ('blk', 'inner')), may hold values from -6 to 6
- v_scale: bfloat16 [4, 1024, 12], P('dp', ('blk', 'inner')), may hold values from 0.5 to 2
- d_out: bfloat16 [4, 1024, 1536], P('dp', ('blk', 'inner')), may hold values from -45 to 45
- q_gain: float32 [128], replicated, may hold values from 0.1 to 1.9
- k_gain: float32 [128], replicated, may hold values from 0.1 to 1.9
- segment_ids: int32 [4, 1024], P('dp'), may hold values from 0 to 63, never falling along the last dimension, each value on 1 to 32 neighbouring positions
Outputs:
- attended: bfloat16 [4, 1024, 1536], P('dp', ('blk', 'inner'))
- d_queries: bfloat16 [4, 1024, 1536], P('dp', ('blk', 'inner'))
- d_keys: bfloat16 [4, 1024, 1536], P('dp', ('blk', 'inner'))
- d_values: bfloat16 [4, 1024, 1536], P('dp', ('blk', 'inner'))
- d_q_gain: float32 [128], replicated
- d_k_gain: float32 [128], replicated
Inputs may be any that keep to these rules, and one draw needn't show every extreme that they name: `segment_ids`: segment numbers never fall along a sequence; every segment has between 1 and 32 tokens and some segment has exactly 32.
All inputs are finite; a program needn't handle non-finite values.
Results may differ from a plain program's by a relative error of at most 0.0086.
Values may be sent and summed in bfloat16 or wider, within the bound.
A program may use at most 64 MiB of HBM per device.

v0:
```python
import functools
import math

import jax
import jax.numpy as jnp
from jax import lax
from jax.experimental import pallas as pl
from jax.experimental.pallas import tpu as pltpu
from jax.sharding import PartitionSpec as P

EPSILON = 1e-06
MESH = pl.DeviceIdType.MESH
AXES = ("dp", "blk", "inner")
F32 = jnp.float32
BF16 = jnp.bfloat16
NT = (((1,), (1,)), ((), ()))
NN = (((1,), (0,)), ((), ()))
TN = (((0,), (0,)), ((), ()))


def dot(a, b, dims):
    return lax.dot_general(a, b, dims, preferred_element_type=F32)


def unit(x):
    inverse = lax.rsqrt(jnp.mean(x * x, axis=-1, keepdims=True) + EPSILON)
    return x * inverse, inverse


def norm_back(d_norm, unit_rows, inverse, gain):
    d_unit = d_norm * gain
    mean = jnp.mean(d_unit * unit_rows, axis=-1, keepdims=True)
    return inverse * (d_unit - unit_rows * mean)


def attend(q_norm, k_norm, v_deq, grad, same, scale):
    e = jnp.where(same, jnp.exp(dot(k_norm, q_norm, NT) * scale), 0.0)
    w = e * (1.0 / jnp.sum(e, axis=0, keepdims=True))
    w_b = w.astype(BF16)
    d_w = dot(v_deq, grad, NT)
    out_dot = jnp.sum(w * d_w, axis=0, keepdims=True)
    d_s = (w * (d_w - out_dot)).astype(BF16)
    return (
        dot(w_b, v_deq, TN),
        dot(d_s, k_norm, TN) * scale,
        dot(d_s, q_norm, NN) * scale,
        dot(w_b, grad, NN),
    )


def to_column(row):
    n = row.shape[1]
    r = lax.broadcasted_iota(jnp.int32, (n, n), 0)
    c = lax.broadcasted_iota(jnp.int32, (n, n), 1)
    return jnp.sum(jnp.where(r == c, row, 0.0), axis=1, keepdims=True)


def kernel(cfg, q_hbm, k_hbm, v_hbm, s_ref, g_hbm, qg_ref, kg_ref, seg_ref,
           att_o, dq_o, dk_o, dv_o, gq_o, gk_o,
           qv, kv, vv, gv, vd, halo, gsrc, gslot,
           load_sem, send_sem, recv_sem, gsend, grecv):
    sizes, rows, heads, hd, h, hpc = cfg
    n_dp, n_blk, n_inner = sizes
    nc = heads // hpc
    width = hpc * hd
    scale = 1.0 / math.sqrt(hd)
    blk, inner = lax.axis_index("blk"), lax.axis_index("inner")
    p = blk * n_inner + inner
    last = n_blk * n_inner - 1
    has_left, has_right = p > 0, p < last
    left, right = p - 1, p + 1

    def at(pos):
        return {"blk": pos // n_inner, "inner": lax.rem(pos, n_inner)}

    loads = [
        pltpu.make_async_copy(src, dst, load_sem.at[i])
        for i, (src, dst) in enumerate(((v_hbm, vv), (q_hbm, qv), (k_hbm, kv), (g_hbm, gv)))
    ]
    for c in loads:
        c.start()

    barrier = pltpu.get_barrier_semaphore()
    for axis, n in zip(AXES, sizes):
        me = lax.axis_index(axis)
        for d in range(1, n):
            pl.semaphore_signal(barrier, inc=1, device_id={axis: lax.rem(me + d, n)},
                                device_id_type=MESH)

    @pl.when(has_left)
    def _():
        pl.semaphore_signal(barrier, inc=1, device_id=at(left), device_id_type=MESH)

    @pl.when(has_right)
    def _():
        pl.semaphore_signal(barrier, inc=1, device_id=at(right), device_id_type=MESH)

    lane = lax.broadcasted_iota(jnp.int32, (rows, heads), 1)
    s_f = s_ref[...].astype(F32)

    def scale_of(head):
        return jnp.sum(jnp.where(lane == head, s_f, 0.0), axis=1, keepdims=True)

    loads[0].wait()
    for head in range(heads):
        cols = slice(head * hd, (head + 1) * hd)
        vd[:, cols] = (vv[:, cols].astype(F32) * s_f[:, head:head + 1]).astype(BF16)

    def seg_at(pos):
        start = pl.multiple_of(pos * rows, 128)
        return seg_ref[:, pl.ds(start, rows)].astype(F32)

    own = seg_at(p)
    prev = jnp.where(has_left, seg_at(jnp.maximum(left, 0)), -1.0)
    nxt = jnp.where(has_right, seg_at(jnp.minimum(right, last)), -2.0)
    own_col = to_column(own)
    edge = jnp.concatenate(
        [prev[:, rows - h:], own[:, :h], own[:, rows - h:], nxt[:, :h]], axis=1)
    edge_col = to_column(edge)
    same_own = own_col == own
    same_edge = edge_col == edge
    before = jnp.sum(prev[:, rows - 1:], axis=1, keepdims=True)
    after = jnp.sum(nxt[:, :1], axis=1, keepdims=True)
    inside = jnp.where((own_col == before) | (own_col == after), 0.0, 1.0)
    split_lo = own_col[:h] == before
    split_hi = own_col[rows - h:] == after
    split_f = 1.0 - jnp.concatenate([inside[:h], inside[rows - h:]], axis=0)

    pl.semaphore_wait(barrier, sum(sizes) - len(sizes)
                      + has_left.astype(jnp.int32) + has_right.astype(jnp.int32))

    srcs = (k_hbm, q_hbm, vd, g_hbm)

    def remote(side, i, c):
        if isinstance(c, int):
            cols = slice(c * width, (c + 1) * width)
        else:
            cols = pl.ds(pl.multiple_of(c * width, 128), width)
        own_rows = slice(0, h) if side == 0 else slice(rows - h, rows)
        return pltpu.make_async_remote_copy(
            src_ref=srcs[i].at[own_rows, cols],
            dst_ref=halo.at[i, 1 - side, :, cols],
            send_sem=send_sem.at[side, i, c],
            recv_sem=recv_sem.at[1 - side, i, c],
            device_id=at(left if side == 0 else right),
            device_id_type=MESH,
        )

    def receive(side, i, c):
        cols = pl.ds(pl.multiple_of(c * width, 128), width)
        return pltpu.make_async_remote_copy(
            src_ref=halo.at[i, side, :, cols],
            dst_ref=halo.at[i, side, :, cols],
            send_sem=send_sem.at[side, i, c],
            recv_sem=recv_sem.at[side, i, c],
            device_id=at(left if side == 0 else right),
            device_id_type=MESH,
        )

    sides = ((0, has_left), (1, has_right))
    for c in range(nc):
        for side, there in sides:
            @pl.when(there)
            def _():
                for i in range(4):
                    remote(side, i, c).start()

    for side, there in sides:
        @pl.when(jnp.logical_not(there))
        def _():
            halo[:, side] = jnp.zeros((4, h, heads * hd), BF16)

    q_gain, k_gain = qg_ref[...], kg_ref[...]
    for c in loads[1:]:
        c.wait()

    def own_step(c, acc):
        acc_q, acc_k = acc
        for j in range(hpc):
            head = c * hpc + j
            cols = pl.ds(pl.multiple_of(head * hd, 128), hd)
            q_unit, q_inv = unit(qv[:, cols].astype(F32))
            k_unit, k_inv = unit(kv[:, cols].astype(F32))
            out, d_q, d_k, d_v = attend(
                (q_unit * q_gain).astype(BF16), (k_unit * k_gain).astype(BF16),
                vd[:, cols], gv[:, cols], same_own, scale)
            att_o[:, cols] = out.astype(BF16)
            dq_o[:, cols] = norm_back(d_q, q_unit, q_inv, q_gain).astype(BF16)
            dk_o[:, cols] = norm_back(d_k, k_unit, k_inv, k_gain).astype(BF16)
            dv_o[:, cols] = (d_v * scale_of(head)).astype(BF16)
            acc_q = acc_q + jnp.sum(d_q * q_unit * inside, axis=0, keepdims=True)
            acc_k = acc_k + jnp.sum(d_k * k_unit * inside, axis=0, keepdims=True)
        return acc_q, acc_k

    zero = jnp.zeros((1, hd), F32)
    acc = lax.fori_loop(0, nc, own_step, (zero, zero))

    def joined(i, ref, cols):
        return jnp.concatenate(
            [halo[i, 0, :, cols], ref[0:h, cols], ref[rows - h:rows, cols], halo[i, 1, :, cols]],
            axis=0)

    def put(ref, cols, value):
        ref[0:h, cols] = jnp.where(split_lo, value[:h].astype(F32),
                                   ref[0:h, cols].astype(F32)).astype(BF16)
        ref[rows - h:rows, cols] = jnp.where(split_hi, value[h:].astype(F32),
                                             ref[rows - h:rows, cols].astype(F32)).astype(BF16)

    def edge_step(c, acc):
        acc_q, acc_k = acc
        for side, there in sides:
            @pl.when(there)
            def _():
                for i in range(4):
                    receive(side, i, c).wait_recv()
        for j in range(hpc):
            head = c * hpc + j
            cols = pl.ds(pl.multiple_of(head * hd, 128), hd)
            q_unit, q_inv = unit(joined(1, qv, cols).astype(F32))
            k_unit, k_inv = unit(joined(0, kv, cols).astype(F32))
            out, d_q, d_k, d_v = attend(
                (q_unit * q_gain).astype(BF16), (k_unit * k_gain).astype(BF16),
                joined(2, vd, cols), joined(3, gv, cols), same_edge, scale)
            mid = slice(h, 3 * h)
            d_q, d_k, q_unit, k_unit = d_q[mid], d_k[mid], q_unit[mid], k_unit[mid]
            s_all = scale_of(head)
            s_mid = jnp.concatenate([s_all[:h], s_all[rows - h:]], axis=0)
            put(att_o, cols, out[mid])
            put(dq_o, cols, norm_back(d_q, q_unit, q_inv[mid], q_gain))
            put(dk_o, cols, norm_back(d_k, k_unit, k_inv[mid], k_gain))
            put(dv_o, cols, d_v[mid] * s_mid)
            acc_q = acc_q + jnp.sum(jnp.where(split_f > 0.5, d_q * q_unit, 0.0), axis=0, keepdims=True)
            acc_k = acc_k + jnp.sum(jnp.where(split_f > 0.5, d_k * k_unit, 0.0), axis=0, keepdims=True)
        return acc_q, acc_k

    acc_q, acc_k = lax.fori_loop(0, nc, edge_step, acc)

    row = lax.broadcasted_iota(jnp.int32, (8, hd), 0)
    total = jnp.where(row == 0, acc_q, jnp.where(row == 1, acc_k, 0.0))
    offset = 0
    for stage, (axis, n) in enumerate(zip(AXES, sizes)):
        me = lax.axis_index(axis)
        gsrc[stage] = total
        gslot[offset + me] = total

        def gain_copy(d, slot, to):
            return pltpu.make_async_remote_copy(
                src_ref=gsrc.at[stage], dst_ref=gslot.at[offset + slot],
                send_sem=gsend.at[offset + d], recv_sem=grecv.at[offset + d],
                device_id={axis: to}, device_id_type=MESH)

        for d in range(1, n):
            gain_copy(d, me, lax.rem(me + d, n)).start()
        for d in range(1, n):
            gain_copy(d, lax.rem(me - d + n, n), lax.rem(me + d, n)).wait()
        total = gslot[offset]
        for i in range(1, n):
            total = total + gslot[offset + i]
        offset += n
    gq_o[...] = total[0:1]
    gk_o[...] = total[1:2]

    for c in range(nc):
        for side, there in sides:
            @pl.when(there)
            def _():
                for i in range(4):
                    remote(side, i, c).wait_send()


def local(queries, keys, values, v_scale, d_out, q_gain, k_gain, segment_ids):
    _, rows, cols = queries.shape
    hd = q_gain.shape[0]
    heads = cols // hd
    sizes = tuple(lax.axis_size(a) for a in AXES)
    h = rows * sizes[2] // 8
    hpc = 3 if heads % 3 == 0 else 1
    nc = heads // hpc
    flat = lambda x: x.reshape(rows, x.shape[2])
    vmem = pl.BlockSpec(memory_space=pltpu.VMEM)
    hbm = pl.BlockSpec(memory_space=pl.ANY)
    big = jax.ShapeDtypeStruct((rows, cols), BF16)
    small = jax.ShapeDtypeStruct((1, hd), F32)
    slots = sum(sizes)
    outs = pl.pallas_call(
        functools.partial(kernel, (sizes, rows, heads, hd, h, hpc)),
        out_shape=(big, big, big, big, small, small),
        in_specs=[hbm, hbm, hbm, vmem, hbm, vmem, vmem, vmem],
        out_specs=(vmem,) * 6,
        scratch_shapes=[
            pltpu.VMEM((rows, cols), BF16),
            pltpu.VMEM((rows, cols), BF16),
            pltpu.VMEM((rows, cols), BF16),
            pltpu.VMEM((rows, cols), BF16),
            pltpu.VMEM((rows, cols), BF16),
            pltpu.VMEM((4, 2, h, cols), BF16),
            pltpu.VMEM((3, 8, hd), F32),
            pltpu.VMEM((slots, 8, hd), F32),
            pltpu.SemaphoreType.DMA((4,)),
            pltpu.SemaphoreType.DMA((2, 4, nc)),
            pltpu.SemaphoreType.DMA((2, 4, nc)),
            pltpu.SemaphoreType.DMA((slots,)),
            pltpu.SemaphoreType.DMA((slots,)),
        ],
        compiler_params=pltpu.CompilerParams(
            collective_id=0, has_side_effects=True, vmem_limit_bytes=32 << 20),
    )(flat(queries), flat(keys), flat(values), flat(v_scale), flat(d_out),
      q_gain.reshape(1, hd), k_gain.reshape(1, hd), segment_ids)
    wide = tuple(x.reshape(1, rows, cols) for x in outs[:4])
    return wide + (outs[4].reshape(hd), outs[5].reshape(hd))


def solution(mesh):
    tokens = P("dp", ("blk", "inner"), None)
    return jax.shard_map(
        local,
        mesh=mesh,
        in_specs=(tokens,) * 5 + (P(), P(), P("dp", None)),
        out_specs=(tokens,) * 4 + (P(), P()),
        check_vma=False,
    )
```

profile of v0, /device:TPU:0, one launch (start us, length us, event | category | flops | bytes accessed | tf_op | source)
XLA Modules:
  0.0 44.2 jit_solution(6487639701818398013)
XLA Ops:
  0.6 0.0 copy-start.7
  0.6 0.7 %copy-done.7 = bf16[1,128,12]{1,2,0:T(8,128)(2,1)S(1)} copy-done((bf16[1,128,12]{1,2,0:T(8,128)(2,1)S(1)}, bf16[1,128,12]{1,2,0:T(8,128)(2,1)}, u32[]{:S(2)}) %copy-start.7) | copy-done | bytes 3096
  1.3 0.0 copy-start.4
  1.3 0.1 copy.14
  1.5 0.0 copy-start.5
  1.5 0.0 copy-start.6
  1.5 0.5 %copy-done.4 = s32[1,1024]{1,0:T(1,128)S(1)} copy-done((s32[1,1024]{1,0:T(1,128)S(1)}, s32[1,1024]{1,0:T(1,128)}, u32[]{:S(2)}) %copy-start.4) | copy-done | bytes 4120
  2.0 0.1 copy-done.5
  2.1 0.0 copy-done.6
  2.1 0.0 copy-start
  2.1 1.0 %copy-done = bf16[1,128,1536]{2,1,0:T(8,128)(2,1)S(1)} copy-done((bf16[1,128,1536]{2,1,0:T(8,128)(2,1)S(1)}, bf16[1,128,1536]{2,1,0:T(8,128)(2,1)}, u32[]{:S(2)}) %copy-start) | copy-done | bytes 393240
  3.1 0.0 copy-start.1
  3.1 1.0 %copy-done.1 = bf16[1,128,1536]{2,1,0:T(8,128)(2,1)S(1)} copy-done((bf16[1,128,1536]{2,1,0:T(8,128)(2,1)S(1)}, bf16[1,128,1536]{2,1,0:T(8,128)(2,1)}, u32[]{:S(2)}) %copy-start.1) | copy-done | bytes 393240
  4.1 0.0 copy-start.2
  4.1 1.0 %copy-done.2 = bf16[1,128,1536]{2,1,0:T(8,128)(2,1)S(1)} copy-done((bf16[1,128,1536]{2,1,0:T(8,128)(2,1)S(1)}, bf16[1,128,1536]{2,1,0:T(8,128)(2,1)}, u32[]{:S(2)}) %copy-start.2) | copy-done | bytes 393240
  5.1 0.0 copy-start.3
  5.1 1.0 %copy-done.3 = bf16[1,128,1536]{2,1,0:T(8,128)(2,1)S(1)} copy-done((bf16[1,128,1536]{2,1,0:T(8,128)(2,1)S(1)}, bf16[1,128,1536]{2,1,0:T(8,128)(2,1)}, u32[]{:S(2)}) %copy-start.3) | copy-done | bytes 393240
  6.1 34.1 %shard_map.127 = (bf16[128,1536]{1,0:T(8,128)(2,1)S(1)}, bf16[128,1536]{1,0:T(8,128)(2,1)S(1)}, bf16[128,1536]{1,0:T(8,128)(2,1)S(1)}, bf16[128,1536]{1,0:T(8,12...) custom-call(bf16[128,1536]{1,0:T(8,128)(2,1)S(1)} %bitcast.17, bf16[128,1536]{1,0:T(8,128)(2,1)S(1)} %bitcast.18, ...), custom_call_target="tpu_custom_call" | custom-call | tf_op jit(solution)/shard_map/pallas_call | solution.py:285
  40.2 0.7 %copy.21 = bf16[1,128,1536]{2,1,0:T(8,128)(2,1)} copy(bf16[1,128,1536]{2,1,0:T(8,128)(2,1)S(1)} %bitcast.16) | data formatting | bytes 786432
  41.0 0.7 %copy.22 = bf16[1,128,1536]{2,1,0:T(8,128)(2,1)} copy(bf16[1,128,1536]{2,1,0:T(8,128)(2,1)S(1)} %bitcast.15) | data formatting | bytes 786432
  41.7 0.7 %copy.23 = bf16[1,128,1536]{2,1,0:T(8,128)(2,1)} copy(bf16[1,128,1536]{2,1,0:T(8,128)(2,1)S(1)} %bitcast.14) | data formatting | bytes 786432
  42.5 0.7 %copy.24 = bf16[1,128,1536]{2,1,0:T(8,128)(2,1)} copy(bf16[1,128,1536]{2,1,0:T(8,128)(2,1)S(1)} %bitcast.13) | data formatting | bytes 786432
  43.2 0.5 %copy.25 = f32[128]{0:T(128)} copy(f32[128]{0:T(128)S(1)} %bitcast.25) | data formatting | bytes 1024
  43.7 0.5 %copy.26 = f32[128]{0:T(128)} copy(f32[128]{0:T(128)S(1)} %bitcast.24) | data formatting | bytes 1024
Async XLA Ops:
  0.6 0.7 %copy-start.7 = (bf16[1,128,12]{1,2,0:T(8,128)(2,1)S(1)}, bf16[1,128,12]{1,2,0:T(8,128)(2,1)}, u32[]{:S(2)}) copy-start(bf16[1,128,12]{1,2,0:T(8,128)(2,1)} %param.11) | copy-start | bytes 9220
  1.3 0.7 %copy-start.4 = (s32[1,1024]{1,0:T(1,128)S(1)}, s32[1,1024]{1,0:T(1,128)}, u32[]{:S(2)}) copy-start(s32[1,1024]{1,0:T(1,128)} %seg_ref.1) | copy-start | bytes 12292
  1.5 0.7 %copy-start.5 = (f32[128]{0:T(128)S(1)}, f32[128]{0:T(128)}, u32[]{:S(2)}) copy-start(f32[128]{0:T(128)} %param.13) | copy-start | bytes 1540
  1.5 0.7 %copy-start.6 = (f32[128]{0:T(128)S(1)}, f32[128]{0:T(128)}, u32[]{:S(2)}) copy-start(f32[128]{0:T(128)} %param.14) | copy-start | bytes 1540
  2.1 1.0 %copy-start = (bf16[1,128,1536]{2,1,0:T(8,128)(2,1)S(1)}, bf16[1,128,1536]{2,1,0:T(8,128)(2,1)}, u32[]{:S(2)}) copy-start(bf16[1,128,1536]{2,1,0:T(8,128)(2,1)} %param.8) | copy-start | bytes 1179652
  3.1 1.0 %copy-start.1 = (bf16[1,128,1536]{2,1,0:T(8,128)(2,1)S(1)}, bf16[1,128,1536]{2,1,0:T(8,128)(2,1)}, u32[]{:S(2)}) copy-start(bf16[1,128,1536]{2,1,0:T(8,128)(2,1)} %param.9) | copy-start | bytes 1179652
  4.1 1.0 %copy-start.2 = (bf16[1,128,1536]{2,1,0:T(8,128)(2,1)S(1)}, bf16[1,128,1536]{2,1,0:T(8,128)(2,1)}, u32[]{:S(2)}) copy-start(bf16[1,128,1536]{2,1,0:T(8,128)(2,1)} %param.10) | copy-start | bytes 1179652
  5.1 1.0 %copy-start.3 = (bf16[1,128,1536]{2,1,0:T(8,128)(2,1)S(1)}, bf16[1,128,1536]{2,1,0:T(8,128)(2,1)}, u32[]{:S(2)}) copy-start(bf16[1,128,1536]{2,1,0:T(8,128)(2,1)} %param.12) | copy-start | bytes 1179652
where the time goes:
time: 44.6 us; the launch traced here: 44.2 us
  Pallas kernels  34.1 us (76%)
  local copies, waits for them, and re-layouts  9.46 us (21%)
  between operations  0.67 us (2%)
    pallas_call x1, Pallas kernels, local(): pl.pallas_call(functools.partial(kernel, (sizes, rows, heads, hd, h, hpc)...  34.1 us
    unnamed x23, local copies, waits for them, and re-layouts  9.46 us

commit v1 on v0

--- a/solution.py
+++ b/solution.py
@@ -55,9 +55,36 @@
     return jnp.sum(jnp.where(r == c, row, 0.0), axis=1, keepdims=True)
 
 
-def kernel(cfg, q_hbm, k_hbm, v_hbm, s_ref, g_hbm, qg_ref, kg_ref, seg_ref,
+def transposed(x):
+    n = x.shape[1]
+    r = lax.broadcasted_iota(jnp.int32, (n, n), 0)
+    c = lax.broadcasted_iota(jnp.int32, (n, n), 1)
+    return dot((r == c).astype(F32).astype(BF16), x, NT)
+
+
+def store(*refs):
+    n = len(refs) // 2
+    sem = refs[-1]
+    copies = [pltpu.make_async_copy(refs[i], refs[n + i], sem.at[i]) for i in range(n)]
+    for c in copies:
+        c.start()
+    for c in copies:
+        c.wait()
+
+
+def grouped(sizes):
+    groups = []
+    for axis, n in zip(AXES, sizes):
+        if groups and groups[-1][1] * n <= 32:
+            groups[-1] = (groups[-1][0] + (axis,), groups[-1][1] * n)
+        else:
+            groups.append(((axis,), n))
+    return groups
+
+
+def kernel(cfg, q_hbm, k_hbm, v_hbm, s_hbm, g_hbm, qg_hbm, kg_hbm, seg_hbm,
            att_o, dq_o, dk_o, dv_o, gq_o, gk_o,
-           qv, kv, vv, gv, vd, halo, gsrc, gslot,
+           qv, kv, vv, gv, s_ref, qg_ref, kg_ref, seg_ref, vd, halo, gsrc, gslot,
            load_sem, send_sem, recv_sem, gsend, grecv):
     sizes, rows, heads, hd, h, hpc = cfg
     n_dp, n_blk, n_inner = sizes
@@ -70,21 +97,38 @@
     has_left, has_right = p > 0, p < last
     left, right = p - 1, p + 1
 
+    size_of = dict(zip(AXES, sizes))
+    stages = grouped(sizes)
+
+    def place(axes):
+        index = 0
+        for axis in axes:
+            index = index * size_of[axis] + lax.axis_index(axis)
+        return index
+
+    def member(axes, index):
+        device = {}
+        for axis in reversed(axes):
+            device[axis] = lax.rem(index, size_of[axis])
+            index = index // size_of[axis]
+        return device
+
     def at(pos):
         return {"blk": pos // n_inner, "inner": lax.rem(pos, n_inner)}
 
     loads = [
         pltpu.make_async_copy(src, dst, load_sem.at[i])
-        for i, (src, dst) in enumerate(((v_hbm, vv), (q_hbm, qv), (k_hbm, kv), (g_hbm, gv)))
+        for i, (src, dst) in enumerate(((s_hbm, s_ref), (v_hbm, vv), (seg_hbm, seg_ref), (qg_hbm, qg_ref),
+                                   (kg_hbm, kg_ref), (q_hbm, qv), (k_hbm, kv), (g_hbm, gv)))
     ]
     for c in loads:
         c.start()
 
     barrier = pltpu.get_barrier_semaphore()
-    for axis, n in zip(AXES, sizes):
-        me = lax.axis_index(axis)
+    for axes, n in stages:
+        me = place(axes)
         for d in range(1, n):
-            pl.semaphore_signal(barrier, inc=1, device_id={axis: lax.rem(me + d, n)},
+            pl.semaphore_signal(barrier, inc=1, device_id=member(axes, lax.rem(me + d, n)),
                                 device_id_type=MESH)
 
     @pl.when(has_left)
@@ -96,12 +140,13 @@
         pl.semaphore_signal(barrier, inc=1, device_id=at(right), device_id_type=MESH)
 
     lane = lax.broadcasted_iota(jnp.int32, (rows, heads), 1)
-    s_f = s_ref[...].astype(F32)
+    loads[0].wait()
+    s_f = transposed(s_ref[...])
 
     def scale_of(head):
         return jnp.sum(jnp.where(lane == head, s_f, 0.0), axis=1, keepdims=True)
 
-    loads[0].wait()
+    loads[1].wait()
     for head in range(heads):
         cols = slice(head * hd, (head + 1) * hd)
         vd[:, cols] = (vv[:, cols].astype(F32) * s_f[:, head:head + 1]).astype(BF16)
@@ -110,6 +155,7 @@
         start = pl.multiple_of(pos * rows, 128)
         return seg_ref[:, pl.ds(start, rows)].astype(F32)
 
+    loads[2].wait()
     own = seg_at(p)
     prev = jnp.where(has_left, seg_at(jnp.maximum(left, 0)), -1.0)
     nxt = jnp.where(has_right, seg_at(jnp.minimum(right, last)), -2.0)
@@ -126,7 +172,7 @@
     split_hi = own_col[rows - h:] == after
     split_f = 1.0 - jnp.concatenate([inside[:h], inside[rows - h:]], axis=0)
 
-    pl.semaphore_wait(barrier, sum(sizes) - len(sizes)
+    pl.semaphore_wait(barrier, sum(n - 1 for _, n in stages)
                       + has_left.astype(jnp.int32) + has_right.astype(jnp.int32))
 
     srcs = (k_hbm, q_hbm, vd, g_hbm)
@@ -170,9 +216,9 @@
         def _():
             halo[:, side] = jnp.zeros((4, h, heads * hd), BF16)
 
+    for c in loads[3:]:
+        c.wait()
     q_gain, k_gain = qg_ref[...], kg_ref[...]
-    for c in loads[1:]:
-        c.wait()
 
     def own_step(c, acc):
         acc_q, acc_k = acc
@@ -235,11 +281,10 @@
 
     acc_q, acc_k = lax.fori_loop(0, nc, edge_step, acc)
 
-    row = lax.broadcasted_iota(jnp.int32, (8, hd), 0)
-    total = jnp.where(row == 0, acc_q, jnp.where(row == 1, acc_k, 0.0))
+    total = jnp.concatenate([acc_q, acc_k], axis=0)
     offset = 0
-    for stage, (axis, n) in enumerate(zip(AXES, sizes)):
-        me = lax.axis_index(axis)
+    for stage, (axes, n) in enumerate(stages):
+        me = place(axes)
         gsrc[stage] = total
         gslot[offset + me] = total
 
@@ -247,7 +292,7 @@
             return pltpu.make_async_remote_copy(
                 src_ref=gsrc.at[stage], dst_ref=gslot.at[offset + slot],
                 send_sem=gsend.at[offset + d], recv_sem=grecv.at[offset + d],
-                device_id={axis: to}, device_id_type=MESH)
+                device_id=member(axes, to), device_id_type=MESH)
 
         for d in range(1, n):
             gain_copy(d, me, lax.rem(me + d, n)).start()
@@ -278,25 +323,29 @@
     nc = heads // hpc
     flat = lambda x: x.reshape(rows, x.shape[2])
     vmem = pl.BlockSpec(memory_space=pltpu.VMEM)
-    hbm = pl.BlockSpec(memory_space=pl.ANY)
+    hbm = pl.BlockSpec(memory_space=pltpu.HBM)
     big = jax.ShapeDtypeStruct((rows, cols), BF16)
     small = jax.ShapeDtypeStruct((1, hd), F32)
-    slots = sum(sizes)
+    slots = sum(n for _, n in grouped(sizes))
     outs = pl.pallas_call(
         functools.partial(kernel, (sizes, rows, heads, hd, h, hpc)),
         out_shape=(big, big, big, big, small, small),
-        in_specs=[hbm, hbm, hbm, vmem, hbm, vmem, vmem, vmem],
+        in_specs=[hbm] * 8,
         out_specs=(vmem,) * 6,
         scratch_shapes=[
             pltpu.VMEM((rows, cols), BF16),
             pltpu.VMEM((rows, cols), BF16),
             pltpu.VMEM((rows, cols), BF16),
             pltpu.VMEM((rows, cols), BF16),
+            pltpu.VMEM((heads, rows), BF16),
+            pltpu.VMEM((1, hd), F32),
+            pltpu.VMEM((1, hd), F32),
+            pltpu.VMEM(segment_ids.shape, jnp.int32),
             pltpu.VMEM((rows, cols), BF16),
             pltpu.VMEM((4, 2, h, cols), BF16),
-            pltpu.VMEM((3, 8, hd), F32),
-            pltpu.VMEM((slots, 8, hd), F32),
-            pltpu.SemaphoreType.DMA((4,)),
+            pltpu.VMEM((3, 2, hd), F32),
+            pltpu.VMEM((slots, 2, hd), F32),
+            pltpu.SemaphoreType.DMA((8,)),
             pltpu.SemaphoreType.DMA((2, 4, nc)),
             pltpu.SemaphoreType.DMA((2, 4, nc)),
             pltpu.SemaphoreType.DMA((slots,)),
@@ -304,8 +353,15 @@
         ],
         compiler_params=pltpu.CompilerParams(
             collective_id=0, has_side_effects=True, vmem_limit_bytes=32 << 20),
-    )(flat(queries), flat(keys), flat(values), flat(v_scale), flat(d_out),
-      q_gain.reshape(1, hd), k_gain.reshape(1, hd), segment_ids)
+    )(*map(lambda x: pltpu.with_memory_space_constraint(x, pltpu.HBM), (flat(queries), flat(keys), flat(values), flat(v_scale).T, flat(d_out),
+      q_gain.reshape(1, hd), k_gain.reshape(1, hd), segment_ids)))
+    outs = pl.pallas_call(
+        store,
+        out_shape=(big, big, big, big, small, small),
+        in_specs=[vmem] * 6,
+        out_specs=(hbm,) * 6,
+        scratch_shapes=[pltpu.SemaphoreType.DMA((6,))],
+    )(*map(lambda x: pltpu.with_memory_space_constraint(x, pltpu.VMEM), outs))
     wide = tuple(x.reshape(1, rows, cols) for x in outs[:4])
     return wide + (outs[4].reshape(hd), outs[5].reshape(hd))
 

time: 44.6 us -> 33.8 us (0.76)
  local copies, waits for them, and re-layouts: 9.46 us -> 0 us
  Pallas kernels: 34.1 us -> 33 us
    unnamed x23 -> x0, local copies, waits for them, and re-layouts: 9.46 us -> none
    pallas_call x1, Pallas kernels: 34.1 us -> 31.8 us  [local(): pl.pallas_call(functools.partial(kernel, (sizes, rows, heads, hd, h, hpc)...]
    pallas_call x0 -> x1, Pallas kernels: none -> 1.19 us  [local(): pl.pallas_call(store, out_shape=(big, big, big, big, small, small), in_sp...]
where the time goes in v1:
time: 33.8 us; the launch traced here: 33.7 us
  Pallas kernels  33 us (98%)
  between operations  0.64 us (2%)
    pallas_call x1, Pallas kernels, local(): pl.pallas_call(functools.partial(kernel, (sizes, rows, heads, hd, h, hpc)...  31.8 us
    pallas_call x1, Pallas kernels, local(): pl.pallas_call(store, out_shape=(big, big, big, big, small, small), in_sp...  1.19 us

profile of v1, /device:TPU:0, one launch (start us, length us, event | category | flops | bytes accessed | tf_op | source)
XLA Modules:
  0.0 33.7 jit_solution(9200965035980661550)
XLA Ops:
  0.6 31.8 %shard_map.127 = (bf16[128,1536]{1,0:T(8,128)(2,1)S(1)}, bf16[128,1536]{1,0:T(8,128)(2,1)S(1)}, bf16[128,1536]{1,0:T(8,128)(2,1)S(1)}, bf16[128,1536]{1,0:T(8,12...) custom-call(bf16[128,1536]{1,0:T(8,128)(2,1)} %bitcast.15, bf16[128,1536]{1,0:T(8,128)(2,1)} %bitcast.16, ...), custom_call_target="tpu_custom_call" | custom-call | tf_op jit(solution)/shard_map/pallas_call | solution.py:330
  32.5 1.2 %shard_map.128 = (bf16[128,1536]{1,0:T(8,128)(2,1)}, bf16[128,1536]{1,0:T(8,128)(2,1)}, bf16[128,1536]{1,0:T(8,128)(2,1)}, bf16[128,1536]{1,0:T(8,128)(2,1)}, f32[1,128]{1,0:T(1,128)}, /*index=5*/f32[1,128]{1,0:T(1,128)}) custom-call(bf16[128,1536]{1,0:T(8,128)(2,1)S(1)} %get-tuple-element.18.refs_0_, bf16[128,1536]{1,0:T(8,128)(2,1)S(1)} %get-tuple-element.19.refs_1_, ...), custom_call_target="tpu_custom_call" | custom-call | tf_op jit(solution)/shard_map/pallas_call | solution.py:358

commit v2 on v1

--- a/solution.py
+++ b/solution.py
@@ -35,7 +35,8 @@
 
 def attend(q_norm, k_norm, v_deq, grad, same, scale):
     e = jnp.where(same, jnp.exp(dot(k_norm, q_norm, NT) * scale), 0.0)
-    w = e * (1.0 / jnp.sum(e, axis=0, keepdims=True))
+    total = jnp.sum(e, axis=0, keepdims=True)
+    w = e * (1.0 / jnp.where(total == 0.0, 1.0, total))
     w_b = w.astype(BF16)
     d_w = dot(v_deq, grad, NT)
     out_dot = jnp.sum(w * d_w, axis=0, keepdims=True)
@@ -84,11 +85,12 @@
 
 def kernel(cfg, q_hbm, k_hbm, v_hbm, s_hbm, g_hbm, qg_hbm, kg_hbm, seg_hbm,
            att_o, dq_o, dk_o, dv_o, gq_o, gk_o,
-           qv, kv, vv, gv, s_ref, qg_ref, kg_ref, seg_ref, vd, halo, gsrc, gslot,
-           load_sem, send_sem, recv_sem, gsend, grecv):
+           qv, kv, vv, gv, s_ref, qg_ref, kg_ref, seg_ref, vd, near, give, take, gsrc, gslot,
+           load_sem, send_sem, recv_sem, give_sem, take_sem, gsend, grecv):
     sizes, rows, heads, hd, h, hpc = cfg
     n_dp, n_blk, n_inner = sizes
     nc = heads // hpc
+    hh = h // 2
     width = hpc * hd
     scale = 1.0 / math.sqrt(hd)
     blk, inner = lax.axis_index("blk"), lax.axis_index("inner")
@@ -163,29 +165,48 @@
     edge = jnp.concatenate(
         [prev[:, rows - h:], own[:, :h], own[:, rows - h:], nxt[:, :h]], axis=1)
     edge_col = to_column(edge)
-    same_own = own_col == own
-    same_edge = edge_col == edge
-    before = jnp.sum(prev[:, rows - 1:], axis=1, keepdims=True)
-    after = jnp.sum(nxt[:, :1], axis=1, keepdims=True)
+    wide_col = jnp.concatenate([to_column(prev)[rows - hh:], own_col, to_column(nxt)[:hh]], axis=0)
+    same_own = wide_col == own
+
+    def pick(row, index):
+        return jnp.sum(row[:, index:index + 1], axis=1, keepdims=True)
+
+    before, after = pick(prev, rows - 1), pick(nxt, 0)
     inside = jnp.where((own_col == before) | (own_col == after), 0.0, 1.0)
     split_lo = own_col[:h] == before
     split_hi = own_col[rows - h:] == after
     split_f = 1.0 - jnp.concatenate([inside[:h], inside[rows - h:]], axis=0)
+    long_lo = jnp.where(pick(own, hh) == before, 1.0, 0.0)
+    long_hi = jnp.where(pick(own, rows - hh - 1) == after, 1.0, 0.0)
+    long_before = jnp.where(pick(prev, rows - hh - 1) == pick(own, 0), 1.0, 0.0)
+    long_after = jnp.where(pick(nxt, hh) == pick(own, rows - 1), 1.0, 0.0)
+    place_e = lax.broadcasted_iota(jnp.int32, (1, 4 * h), 1)
+    asks = jnp.where(
+        (place_e < hh) | (place_e >= 4 * h - hh), 0.0,
+        jnp.where(place_e < h, 1.0 - long_before,
+                  jnp.where(place_e >= 3 * h, 1.0 - long_after, 1.0)))
+    same_edge = jnp.where(edge_col == edge, asks, 0.0) > 0.5
+    lo_is_long = jnp.broadcast_to(long_lo, (hh, hd)) > 0.5
+    hi_is_long = jnp.broadcast_to(long_hi, (hh, hd)) > 0.5
+    lo_far = jnp.broadcast_to(own_col[hh:h], (hh, hd)) == before
+    hi_far = jnp.broadcast_to(own_col[rows - h:rows - hh], (hh, hd)) == after
+    lo_adds = jnp.where(own_col[:hh] == before, long_before, 0.0)
+    hi_adds = jnp.where(own_col[rows - hh:] == after, long_after, 0.0)
 
     pl.semaphore_wait(barrier, sum(n - 1 for _, n in stages)
                       + has_left.astype(jnp.int32) + has_right.astype(jnp.int32))
 
-    srcs = (k_hbm, q_hbm, vd, g_hbm)
+    srcs = (k_hbm, vd)
+
+    def columns(c):
+        return pl.ds(pl.multiple_of(c * width, 128), width)
 
     def remote(side, i, c):
-        if isinstance(c, int):
-            cols = slice(c * width, (c + 1) * width)
-        else:
-            cols = pl.ds(pl.multiple_of(c * width, 128), width)
-        own_rows = slice(0, h) if side == 0 else slice(rows - h, rows)
+        own_rows = slice(0, hh) if side == 0 else slice(rows - hh, rows)
+        cols = slice(c * width, (c + 1) * width)
         return pltpu.make_async_remote_copy(
             src_ref=srcs[i].at[own_rows, cols],
-            dst_ref=halo.at[i, 1 - side, :, cols],
+            dst_ref=near.at[i, 1 - side, :, cols],
             send_sem=send_sem.at[side, i, c],
             recv_sem=recv_sem.at[1 - side, i, c],
             device_id=at(left if side == 0 else right),
@@ -193,28 +214,48 @@
         )
 
     def receive(side, i, c):
-        cols = pl.ds(pl.multiple_of(c * width, 128), width)
         return pltpu.make_async_remote_copy(
-            src_ref=halo.at[i, side, :, cols],
-            dst_ref=halo.at[i, side, :, cols],
+            src_ref=near.at[i, side, :, columns(c)],
+            dst_ref=near.at[i, side, :, columns(c)],
             send_sem=send_sem.at[side, i, c],
             recv_sem=recv_sem.at[side, i, c],
             device_id=at(left if side == 0 else right),
             device_id_type=MESH,
         )
 
+    def second(side, c):
+        return pltpu.make_async_remote_copy(
+            src_ref=give.at[side, :, :, columns(c)],
+            dst_ref=take.at[1 - side, :, :, columns(c)],
+            send_sem=give_sem.at[side, c],
+            recv_sem=take_sem.at[1 - side, c],
+            device_id=at(left if side == 0 else right),
+            device_id_type=MESH,
+        )
+
+    def second_receive(side, c):
+        return pltpu.make_async_remote_copy(
+            src_ref=take.at[side, :, :, columns(c)],
+            dst_ref=take.at[side, :, :, columns(c)],
+            send_sem=give_sem.at[side, c],
+            recv_sem=take_sem.at[side, c],
+            device_id=at(left if side == 0 else right),
+            device_id_type=MESH,
+        )
+
     sides = ((0, has_left), (1, has_right))
     for c in range(nc):
         for side, there in sides:
             @pl.when(there)
             def _():
-                for i in range(4):
+                for i in range(2):
                     remote(side, i, c).start()
 
     for side, there in sides:
         @pl.when(jnp.logical_not(there))
         def _():
-            halo[:, side] = jnp.zeros((4, h, heads * hd), BF16)
+            near[:, side] = jnp.zeros((2, hh, heads * hd), BF16)
+            take[side] = jnp.zeros((2, hh, heads * hd), BF16)
 
     for c in loads[3:]:
         c.wait()
@@ -222,29 +263,56 @@
 
     def own_step(c, acc):
         acc_q, acc_k = acc
+        for side, there in sides:
+            @pl.when(there)
+            def _():
+                for i in range(2):
+                    receive(side, i, c).wait_recv()
         for j in range(hpc):
             head = c * hpc + j
             cols = pl.ds(pl.multiple_of(head * hd, 128), hd)
-            q_unit, q_inv = unit(qv[:, cols].astype(F32))
-            k_unit, k_inv = unit(kv[:, cols].astype(F32))
+            q, g = qv[:, cols], gv[:, cols]
+            k = jnp.concatenate([near[0, 0, :, cols], kv[:, cols], near[0, 1, :, cols]], axis=0)
+            v = jnp.concatenate([near[1, 0, :, cols], vd[:, cols], near[1, 1, :, cols]], axis=0)
+            k, v_f = k.astype(F32), v.astype(F32)
+            q_f, g_f = q.astype(F32), g.astype(F32)
+            q_unit, q_inv = unit(q_f)
+            k_unit, k_inv = unit(k)
             out, d_q, d_k, d_v = attend(
                 (q_unit * q_gain).astype(BF16), (k_unit * k_gain).astype(BF16),
-                vd[:, cols], gv[:, cols], same_own, scale)
+                v, g, same_own, scale)
+            far, beyond = slice(h, h + hh), slice(hh + rows, rows + h)
+            give[0, 0, :, cols] = jnp.where(
+                lo_is_long, jnp.where(lo_far, k[far], d_k[:hh]), q_f[:hh]).astype(BF16)
+            give[0, 1, :, cols] = jnp.where(
+                lo_is_long, jnp.where(lo_far, v_f[far], d_v[:hh]), g_f[:hh]).astype(BF16)
+            far = slice(rows - hh, rows)
+            give[1, 0, :, cols] = jnp.where(
+                hi_is_long, jnp.where(hi_far, k[far], d_k[beyond]), q_f[rows - hh:]).astype(BF16)
+            give[1, 1, :, cols] = jnp.where(
+                hi_is_long, jnp.where(hi_far, v_f[far], d_v[beyond]), g_f[rows - hh:]).astype(BF16)
+            mid = slice(hh, hh + rows)
+            d_k, d_v, k_unit, k_inv = d_k[mid], d_v[mid], k_unit[mid], k_inv[mid]
             att_o[:, cols] = out.astype(BF16)
             dq_o[:, cols] = norm_back(d_q, q_unit, q_inv, q_gain).astype(BF16)
             dk_o[:, cols] = norm_back(d_k, k_unit, k_inv, k_gain).astype(BF16)
             dv_o[:, cols] = (d_v * scale_of(head)).astype(BF16)
-            acc_q = acc_q + jnp.sum(d_q * q_unit * inside, axis=0, keepdims=True)
-            acc_k = acc_k + jnp.sum(d_k * k_unit * inside, axis=0, keepdims=True)
+            acc_q = acc_q + jnp.sum(jnp.where(inside > 0.5, d_q * q_unit, 0.0), axis=0, keepdims=True)
+            acc_k = acc_k + jnp.sum(jnp.where(inside > 0.5, d_k * k_unit, 0.0), axis=0, keepdims=True)
+        for side, there in sides:
+            @pl.when(there)
+            def _():
+                second(side, c).start()
         return acc_q, acc_k
 
     zero = jnp.zeros((1, hd), F32)
     acc = lax.fori_loop(0, nc, own_step, (zero, zero))
 
-    def joined(i, ref, cols):
+    none = jnp.zeros((hh, hd), BF16)
+
+    def joined(ref, cols, far_lo, near_lo, near_hi, far_hi):
         return jnp.concatenate(
-            [halo[i, 0, :, cols], ref[0:h, cols], ref[rows - h:rows, cols], halo[i, 1, :, cols]],
-            axis=0)
+            [far_lo, near_lo, ref[0:h, cols], ref[rows - h:rows, cols], near_hi, far_hi], axis=0)
 
     def put(ref, cols, value):
         ref[0:h, cols] = jnp.where(split_lo, value[:h].astype(F32),
@@ -257,24 +325,36 @@
         for side, there in sides:
             @pl.when(there)
             def _():
-                for i in range(4):
-                    receive(side, i, c).wait_recv()
+                second_receive(side, c).wait_recv()
         for j in range(hpc):
             head = c * hpc + j
             cols = pl.ds(pl.multiple_of(head * hd, 128), hd)
-            q_unit, q_inv = unit(joined(1, qv, cols).astype(F32))
-            k_unit, k_inv = unit(joined(0, kv, cols).astype(F32))
+            lo_0, lo_1 = take[0, 0, :, cols], take[0, 1, :, cols]
+            hi_0, hi_1 = take[1, 0, :, cols], take[1, 1, :, cols]
+            q_unit, q_inv = unit(joined(qv, cols, none, lo_0, hi_0, none).astype(F32))
+            k_unit, k_inv = unit(joined(
+                kv, cols, lo_0, near[0, 0, :, cols], near[0, 1, :, cols], hi_0).astype(F32))
             out, d_q, d_k, d_v = attend(
                 (q_unit * q_gain).astype(BF16), (k_unit * k_gain).astype(BF16),
-                joined(2, vd, cols), joined(3, gv, cols), same_edge, scale)
+                joined(vd, cols, lo_1, near[1, 0, :, cols], near[1, 1, :, cols], hi_1),
+                joined(gv, cols, none, lo_1, hi_1, none), same_edge, scale)
             mid = slice(h, 3 * h)
-            d_q, d_k, q_unit, k_unit = d_q[mid], d_k[mid], q_unit[mid], k_unit[mid]
+
+            def with_sums(x, lo, hi):
+                return jnp.concatenate(
+                    [x[h:h + hh] + jnp.where(lo_adds > 0.5, lo.astype(F32), 0.0),
+                     x[h + hh:3 * h - hh],
+                     x[3 * h - hh:3 * h] + jnp.where(hi_adds > 0.5, hi.astype(F32), 0.0)], axis=0)
+
+            d_v = with_sums(d_v, lo_1, hi_1)
+            d_k = with_sums(d_k, lo_0, hi_0)
+            d_q, q_unit, k_unit = d_q[mid], q_unit[mid], k_unit[mid]
             s_all = scale_of(head)
             s_mid = jnp.concatenate([s_all[:h], s_all[rows - h:]], axis=0)
             put(att_o, cols, out[mid])
             put(dq_o, cols, norm_back(d_q, q_unit, q_inv[mid], q_gain))
             put(dk_o, cols, norm_back(d_k, k_unit, k_inv[mid], k_gain))
-            put(dv_o, cols, d_v[mid] * s_mid)
+            put(dv_o, cols, d_v * s_mid)
             acc_q = acc_q + jnp.sum(jnp.where(split_f > 0.5, d_q * q_unit, 0.0), axis=0, keepdims=True)
             acc_k = acc_k + jnp.sum(jnp.where(split_f > 0.5, d_k * k_unit, 0.0), axis=0, keepdims=True)
         return acc_q, acc_k
@@ -309,8 +389,9 @@
         for side, there in sides:
             @pl.when(there)
             def _():
-                for i in range(4):
+                for i in range(2):
                     remote(side, i, c).wait_send()
+                second(side, c).wait_send()
 
 
 def local(queries, keys, values, v_scale, d_out, q_gain, k_gain, segment_ids):
@@ -342,12 +423,16 @@
             pltpu.VMEM((1, hd), F32),
             pltpu.VMEM(segment_ids.shape, jnp.int32),
             pltpu.VMEM((rows, cols), BF16),
-            pltpu.VMEM((4, 2, h, cols), BF16),
+            pltpu.VMEM((2, 2, h // 2, cols), BF16),
+            pltpu.VMEM((2, 2, h // 2, cols), BF16),
+            pltpu.VMEM((2, 2, h // 2, cols), BF16),
             pltpu.VMEM((3, 2, hd), F32),
             pltpu.VMEM((slots, 2, hd), F32),
             pltpu.SemaphoreType.DMA((8,)),
-            pltpu.SemaphoreType.DMA((2, 4, nc)),
-            pltpu.SemaphoreType.DMA((2, 4, nc)),
+            pltpu.SemaphoreType.DMA((2, 2, nc)),
+            pltpu.SemaphoreType.DMA((2, 2, nc)),
+            pltpu.SemaphoreType.DMA((2, nc)),
+            pltpu.SemaphoreType.DMA((2, nc)),
             pltpu.SemaphoreType.DMA((slots,)),
             pltpu.SemaphoreType.DMA((slots,)),
         ],

time: 33.8 us -> 28.3 us (0.84)
  Pallas kernels: 33 us -> 27.5 us
    pallas_call x1, Pallas kernels: 31.8 us -> 26.3 us  [local(): pl.pallas_call(functools.partial(kernel, (sizes, rows, heads, hd, h, hpc)...]
where the time goes in v2:
time: 28.3 us; the launch traced here: 28.1 us
  Pallas kernels  27.5 us (97%)
  between operations  0.64 us (2%)
    pallas_call x1, Pallas kernels, local(): pl.pallas_call(functools.partial(kernel, (sizes, rows, heads, hd, h, hpc)...  26.3 us
    pallas_call x1, Pallas kernels, local(): pl.pallas_call(store, out_shape=(big, big, big, big, small, small), in_sp...  1.19 us

profile of v2, /device:TPU:0, one launch (start us, length us, event | category | flops | bytes accessed | tf_op | source)
XLA Modules:
  0.0 28.1 jit_solution(13454691614200287962)
XLA Ops:
  0.6 26.3 %shard_map.127 = (bf16[128,1536]{1,0:T(8,128)(2,1)S(1)}, bf16[128,1536]{1,0:T(8,128)(2,1)S(1)}, bf16[128,1536]{1,0:T(8,128)(2,1)S(1)}, bf16[128,1536]{1,0:T(8,12...) custom-call(bf16[128,1536]{1,0:T(8,128)(2,1)} %bitcast.15, bf16[128,1536]{1,0:T(8,128)(2,1)} %bitcast.16, ...), custom_call_target="tpu_custom_call" | custom-call | tf_op jit(solution)/shard_map/pallas_call | solution.py:411
  26.9 1.2 %shard_map.128 = (bf16[128,1536]{1,0:T(8,128)(2,1)}, bf16[128,1536]{1,0:T(8,128)(2,1)}, bf16[128,1536]{1,0:T(8,128)(2,1)}, bf16[128,1536]{1,0:T(8,128)(2,1)}, f32[1,128]{1,0:T(1,128)}, /*index=5*/f32[1,128]{1,0:T(1,128)}) custom-call(bf16[128,1536]{1,0:T(8,128)(2,1)S(1)} %get-tuple-element.18.refs_0_, bf16[128,1536]{1,0:T(8,128)(2,1)S(1)} %get-tuple-element.19.refs_1_, ...), custom_call_target="tpu_custom_call" | custom-call | tf_op jit(solution)/shard_map/pallas_call | solution.py:443

commit v3 on v2

--- a/solution.py
+++ b/solution.py
@@ -371,13 +371,16 @@
         def gain_copy(d, slot, to):
             return pltpu.make_async_remote_copy(
                 src_ref=gsrc.at[stage], dst_ref=gslot.at[offset + slot],
-                send_sem=gsend.at[offset + d], recv_sem=grecv.at[offset + d],
+                send_sem=gsend.at[stage], recv_sem=grecv.at[stage],
                 device_id=member(axes, to), device_id_type=MESH)
 
         for d in range(1, n):
             gain_copy(d, me, lax.rem(me + d, n)).start()
-        for d in range(1, n):
-            gain_copy(d, lax.rem(me - d + n, n), lax.rem(me + d, n)).wait()
+        everything = gslot.at[pl.ds(offset, n - 1)]
+        pltpu.make_async_remote_copy(
+            src_ref=everything, dst_ref=everything,
+            send_sem=gsend.at[stage], recv_sem=grecv.at[stage],
+            device_id=member(axes, lax.rem(me + 1, n)), device_id_type=MESH).wait()
         total = gslot[offset]
         for i in range(1, n):
             total = total + gslot[offset + i]

time: 28.3 us -> 28.2 us (level)
  no operation moved by 1% of the time
where the time goes in v3:
time: 28.2 us; the launch traced here: 28.1 us
  Pallas kernels  27.5 us (98%)
  between operations  0.64 us (2%)
    pallas_call x1, Pallas kernels, local(): pl.pallas_call(functools.partial(kernel, (sizes, rows, heads, hd, h, hpc)...  26.3 us
    pallas_call x1, Pallas kernels, local(): pl.pallas_call(store, out_shape=(big, big, big, big, small, small), in_sp...  1.19 us

profile of v3, /device:TPU:0, one launch (start us, length us, event | category | flops | bytes accessed | tf_op | source)
XLA Modules:
  0.0 28.1 jit_solution(7602032050949197863)
XLA Ops:
  0.6 26.3 %shard_map.127 = (bf16[128,1536]{1,0:T(8,128)(2,1)S(1)}, bf16[128,1536]{1,0:T(8,128)(2,1)S(1)}, bf16[128,1536]{1,0:T(8,128)(2,1)S(1)}, bf16[128,1536]{1,0:T(8,12...) custom-call(bf16[128,1536]{1,0:T(8,128)(2,1)} %bitcast.15, bf16[128,1536]{1,0:T(8,128)(2,1)} %bitcast.16, ...), custom_call_target="tpu_custom_call" | custom-call | tf_op jit(solution)/shard_map/pallas_call | solution.py:414
  26.9 1.2 %shard_map.128 = (bf16[128,1536]{1,0:T(8,128)(2,1)}, bf16[128,1536]{1,0:T(8,128)(2,1)}, bf16[128,1536]{1,0:T(8,128)(2,1)}, bf16[128,1536]{1,0:T(8,128)(2,1)}, f32[1,128]{1,0:T(1,128)}, /*index=5*/f32[1,128]{1,0:T(1,128)}) custom-call(bf16[128,1536]{1,0:T(8,128)(2,1)S(1)} %get-tuple-element.18.refs_0_, bf16[128,1536]{1,0:T(8,128)(2,1)S(1)} %get-tuple-element.19.refs_1_, ...), custom_call_target="tpu_custom_call" | custom-call | tf_op jit(solution)/shard_map/pallas_call | solution.py:446
